TPU v7x, 32 devices: a whole 2x2x4 slice. The times are simulated.
32 devices in a mesh: dp: 8 (over y, x, core), mp: 4 (over z).
Axes of the slice: x: 2, y: 2, z: 4, core: 2. Of those that a mesh axis runs over, the one named last changes fastest.
Arguments:
- pooled: bfloat16 [2048, 3584], P('dp', 'mp'), may hold values from -4 to 4
- w_out: bfloat16 [3584, 3584], P('mp'), may hold values from -0.028931878 to 0.028931878
- assignments: int32 [2048], P('dp'), may hold values from 0 to 4095
- ema_sums: float32 [4096, 3584], P('mp', 'dp'), may hold values from -0.40089186 to 0.40089186
- ema_counts: float32 [4096], P('mp'), may hold values from 1 to 8
Outputs:
- distances: float32 [2048, 4096], P('dp', 'mp')
- new_sums: float32 [4096, 3584], P('mp', 'dp')
- new_counts: float32 [4096], P('mp')
- new_centroids: bfloat16 [4096, 3584], P('mp', 'dp')
All inputs are finite; a program needn't handle non-finite values.
Results may differ from a plain program's by a relative error of at most 0.0011.
Values may be sent and summed in bfloat16 or wider, within the bound.
A program may use at most 64 MiB of HBM per device.

v0:
```python
import math
import jax
import jax.numpy as jnp
from jax import lax
from jax.sharding import PartitionSpec as P

EPSILON = 1e-06
EMA_DECAY = 0.9


def body(pooled, w_out, assignments, ema_sums, ema_counts):
    partial_value = jnp.dot(pooled, w_out, preferred_element_type=jnp.float32)
    projected = lax.psum(partial_value, "mp")
    inverse_norm = 1.0 / jnp.sqrt(jnp.sum(projected * projected, axis=1, keepdims=True) + EPSILON)
    embedded = (projected * inverse_norm).astype(jnp.bfloat16)
    local_centers = ema_sums.shape[0]
    doc_rows = embedded.shape[0]
    centers = (ema_sums / ema_counts[:, None]).astype(jnp.bfloat16)
    column_piece = lax.all_gather(centers, "dp", axis=1, tiled=True)
    products = lax.dot_general(
        embedded, column_piece, (((1,), (1,)), ((), ())), preferred_element_type=jnp.float32
    )
    piece_wide = column_piece.astype(jnp.float32)
    center_norms = jnp.sum(piece_wide * piece_wide, axis=1)
    products, center_norms = (products, center_norms)
    embed_wide = embedded.astype(jnp.float32)
    doc_norms = jnp.sum(embed_wide * embed_wide, axis=1)
    distances = doc_norms[:, None] + center_norms[None, :] - 2.0 * products
    first_center = lax.axis_index("mp") * local_centers
    center_ids = first_center + jnp.arange(local_centers, dtype=jnp.int32)
    feature_cols = ema_sums.shape[1]
    every_assign = lax.all_gather(assignments, "dp", axis=0, tiled=True)
    own_columns = lax.all_to_all(embedded, "dp", split_axis=1, concat_axis=0, tiled=True)
    shard_count = lax.axis_size("dp")
    group_size = math.gcd(shard_count, max(1, 2048 // doc_rows))
    block_rows = group_size * doc_rows
    turns = shard_count // group_size

    def add_block(block_index, totals):
        sums_now, counts_now = totals
        block_assign = lax.dynamic_slice_in_dim(
            every_assign, block_index * block_rows, block_rows, 0
        )
        block_columns = lax.dynamic_slice_in_dim(
            own_columns, block_index * block_rows, block_rows, 0
        )
        one_hot = (block_assign[None, :] == center_ids[:, None]).astype(jnp.bfloat16)
        sums_now = sums_now + jnp.dot(one_hot, block_columns, preferred_element_type=jnp.float32)
        counts_now = counts_now + jnp.sum(one_hot, axis=1, dtype=jnp.float32)
        return (sums_now, counts_now)

    start_sums = (
        jnp.zeros((local_centers, feature_cols), jnp.float32),
        jnp.zeros((local_centers,), jnp.float32),
    )
    batch_sums, batch_counts = lax.fori_loop(0, turns, add_block, start_sums)
    new_counts = EMA_DECAY * ema_counts + (1.0 - EMA_DECAY) * batch_counts
    new_sums = EMA_DECAY * ema_sums + (1.0 - EMA_DECAY) * batch_sums
    new_centroids = (new_sums / new_counts[:, None]).astype(jnp.bfloat16)
    return (distances, new_sums, new_counts, new_centroids)


def solution(mesh):
    return jax.shard_map(
        body,
        mesh=mesh,
        in_specs=(P("dp", "mp"), P("mp", None), P("dp"), P("mp", "dp"), P("mp")),
        out_specs=(P("dp", "mp"), P("mp", "dp"), P("mp"), P("mp", "dp")),
        check_vma=False,
    )
```

profile of v0, /device:TPU:0, one launch (start us, length us, event | category | flops | bytes accessed | tf_op | source)
XLA Modules:
  0.0 215.6 jit_solution(4043559094026590558)
XLA Ops:
  8.0 0.0 copy-start
  8.0 0.0 all-reduce.2.cloned.1.call-start
  8.1 1.0 copy-done
  9.0 6.8 %fusion.7 = f32[256,3584]{1,0:T(8,128)} fusion(bf16[256,896]{1,0:T(8,128)(2,1)S(1)} %copy-done, bf16[896,3584]{1,0:T(8,128)(2,1)} %param.6), kind=kOutput, calls=%fused_computation.18 | convolution fusion | flops 1644167168 | bytes 10551296 | tf_op jit(solution)/shard_map/dot_general | solution.py:12
  15.8 0.0 copy-start.5
  15.8 0.0 copy-start.7
  15.8 0.0 all-reduce.2.cloned.1.call-update
  15.8 0.0 all-gather.3.cloned.1.call-start
  15.9 1.4 copy-done.5
  17.3 0.0 copy-done.7
  17.3 1.1 divide_convert_fusion.1
  18.5 0.0 all-gather.3.cloned.1.call-update
  18.5 138.3 %all-reduce.2.cloned.1.call-done = f32[256,3584]{1,0:T(8,128)} async-done(((f32[256,3584]{1,0:T(8,128)}), f32[256,3584]{1,0:T(8,128)}) %all-reduce.2.cloned.1.call-update) | async-done | bytes 3670032 | tf_op jit(solution)/shard_map/psum | solution.py:13
  156.7 0.0 copy-start.1
  156.7 2.5 %multiply_reduce_fusion.2 = f32[256]{0:T(256)S(1)} fusion(f32[256,3584]{1,0:T(8,128)} %all-reduce.2.cloned.1.call-done), kind=kLoop, calls=%fused_computation.9 | loop fusion | flops 1834752 | bytes 3671040 | tf_op jit(solution)/shard_map/reduce_sum | solution.py:14
  159.3 0.6 copy-done.1
  159.9 0.6 multiply_reduce_fusion.1
  160.5 0.0 copy-start.3
  160.5 2.5 %copy.13 = bf16[256,3584]{0,1:T(8,128)(2,1)} copy(bf16[256,3584]{1,0:T(8,128)(2,1)S(1)} %get-tuple-element.19) | data formatting | bytes 3670016 | tf_op jit(solution)/shard_map/convert_element_type | solution.py:15
  162.9 0.0 copy-start.9
  162.9 0.0 copy-done.3
  162.9 3.8 %all-to-all-start = ((bf16[256,8,448]{0,2,1:T(8,128)(2,1)}), bf16[256,8,448]{0,2,1:T(8,128)(2,1)S(1)}, u32[]{:S(2)}, u32[]{:S(2)}) async-start(bf16[256,8,448]{0,2,1:T(8,128)(2,1)} %bitcast.12), calls=%async_computation | async-start | bytes 3670016 | tf_op jit(solution)/shard_map/all_to_all | solution.py:33
  166.7 0.0 copy-done.9
  166.7 26.9 %all-gather = s32[8,1,256]{2,1,0:T(1,128)S(1)} all-gather(s32[1,1,256]{2,1,0:T(1,128)S(1)} %bitcast.16), channel_id=1, replica_groups=mesh['dp'=8,'mp'=4] {'dp'}, dimensions={0}, use_global_device_ids=true | all-gather | bytes 9216 | tf_op jit(solution)/shard_map/all_gather | solution.py:32
  193.6 1.0 convert_reduce_fusion
  194.6 0.0 copy-start.8
  194.6 0.0 all-to-all-done
  194.6 0.0 copy-start.6
  194.6 0.2 copy.15
  194.8 1.3 copy-done.6
  196.1 0.0 copy-start.4
  196.1 3.8 %divide_convert_fusion = (bf16[1024,448]{0,1:T(8,128)(2,1)}, f32[1024,448]{0,1:T(8,128)}) fusion(f32[1024]{0:T(1024)S(1)} %multiply_add_fusion.1, bf16[2048,448]{0,1:T(8,128)(2,1)S(1)} %bitcast.13, s32[2048]{0:T(1024)S(1)} %bitcast.15, s32[1024]{0:T(1024)S(1)} %iota_add_fusion, f32[1024,448]{0,1:T(8,128)S(1)} %copy-done.6), kind=kOutput, calls=%fused_computation.10 | convolution fusion | flops 1883439104 | bytes 6438912 | tf_op jit(solution)/shard_map/while/body/eval_jaxpr/dot_general | solution.py:48
  199.9 0.0 copy-done.8
  199.9 0.0 all-gather.3.cloned.1.call-done
  199.9 0.0 copy-start.2
  199.9 4.7 %multiply_reduce_fusion = f32[1024]{0:T(1024)S(1)} fusion(bf16[1024,3584]{0,1:T(8,128)(2,1)} %all-gather.3.cloned.1.call-done), kind=kLoop, calls=%fused_computation | loop fusion | flops 11009024 | bytes 7344128 | tf_op jit(solution)/shard_map/reduce_sum | solution.py:24
  204.6 0.0 copy-done.4
  204.6 0.4 copy-done.2
  205.1 3.0 %fusion.6 = f32[256,1024]{1,0:T(8,128)} fusion(bf16[256,3584]{1,0:T(8,128)(2,1)S(1)} %copy-done.4, bf16[1024,3584]{0,1:T(8,128)(2,1)S(1)} %copy-done.2, f32[1024]{0:T(1024)S(1)} %multiply_reduce_fusion, f32[256]{0:T(256)S(1)} %get-tuple-element.18), kind=kOutput, calls=%fused_computation.14 | convolution fusion | flops 1879834624 | bytes 10228736 | tf_op jit(solution)/shard_map/dot_general | solution.py:20
  (3 shorter events, 0.0 us)
Async XLA Ops:
  8.0 1.0 copy-start
  8.0 148.7 %all-reduce.2.cloned.1.call-start = ((), (), s32[]{:S(2)}) async-start(), calls=%async_computation.1 | async-start | bytes 7340032 | tf_op jit(solution)/shard_map/psum | solution.py:13
  15.8 1.5 copy-start.5
  15.8 1.5 copy-start.7
  15.8 184.1 %all-gather.3.cloned.1.call-start = ((), (), s32[]{:S(2)}) async-start(), calls=%async_computation.2 | async-start | bytes 8257536 | tf_op jit(solution)/shard_map/all_gather | solution.py:19
  156.7 3.1 %copy-start.1 = (f32[256,3584]{1,0:T(8,128)S(1)}, f32[256,3584]{1,0:T(8,128)}, u32[]{:S(2)}) copy-start(f32[256,3584]{1,0:T(8,128)} %all-reduce.2.cloned.1.call-done) | copy-start | bytes 11010052
  160.5 2.5 %copy-start.3 = (bf16[256,3584]{1,0:T(8,128)(2,1)}, bf16[256,3584]{1,0:T(8,128)(2,1)S(1)}, u32[]{:S(2)}) copy-start(bf16[256,3584]{1,0:T(8,128)(2,1)S(1)} %get-tuple-element.19) | copy-start | bytes 5505028
  162.9 3.8 %copy-start.9 = (s32[256]{0:T(256)S(1)}, s32[256]{0:T(256)}, u32[]{:S(2)}) copy-start(s32[256]{0:T(256)} %param.7) | copy-start | bytes 3076
  162.9 31.6 %all-to-all-start = ((bf16[256,8,448]{0,2,1:T(8,128)(2,1)}), bf16[256,8,448]{0,2,1:T(8,128)(2,1)S(1)}, u32[]{:S(2)}, u32[]{:S(2)}) async-start(bf16[256,8,448]{0,2,1:T(8,128)(2,1)} %bitcast.12), calls=%async_computation | async-start | bytes 3670016 | tf_op jit(solution)/shard_map/all_to_all | solution.py:33
  194.6 5.3 %copy-start.8 = (f32[1024]{0:T(1024)}, f32[1024]{0:T(1024)S(1)}, u32[]{:S(2)}) copy-start(f32[1024]{0:T(1024)S(1)} %multiply_add_fusion.1) | copy-start | bytes 12292
  194.6 1.5 copy-start.6
  196.1 8.5 %copy-start.4 = (bf16[256,3584]{1,0:T(8,128)(2,1)S(1)}, bf16[256,3584]{1,0:T(8,128)(2,1)}, u32[]{:S(2)}) copy-start(bf16[256,3584]{1,0:T(8,128)(2,1)} %copy-done.3) | copy-start | bytes 5505028
  199.9 5.2 %copy-start.2 = (bf16[1024,3584]{0,1:T(8,128)(2,1)S(1)}, bf16[1024,3584]{0,1:T(8,128)(2,1)}, u32[]{:S(2)}) copy-start(bf16[1024,3584]{0,1:T(8,128)(2,1)} %all-gather.3.cloned.1.call-done) | copy-start | bytes 22020100
Sparse Core Ops, SparseCore 0:
  16.0 140.7 all-reduce.1
Sparse Core Ops, SparseCore 1:
  18.8 52.4 all-gather.2
where the time goes:
time: 216 us
  waiting for transfers between devices  138 us (64%)
  blocking collectives  26.9 us (12%)
  between operations  15.5 us (7%)
  matrix products  13.6 us (6%)
  other arithmetic  9.94 us (5%)
  local copies, waits for them, and re-layouts  7.42 us (3%)
  starting transfers between devices  3.87 us (2%)
    psum x1, waiting for transfers between devices, body(): projected = lax.psum(partial_value, 'mp')  138 us
    all_gather x1, blocking collectives, body(): every_assign = lax.all_gather(assignments, 'dp', axis=0, tiled=True)  26.9 us
    dot_general x1, matrix products, body(): partial_value = jnp.dot(pooled, w_out, preferred_element_type=jnp.float32)  6.79 us
    reduce_sum x1, other arithmetic, body(): center_norms = jnp.sum(piece_wide * piece_wide, axis=1)  4.74 us
    unnamed x20, local copies, waits for them, and re-layouts  4.72 us
  transfers between devices with their start and end apart: 3, of which 1 were waited for; matrix products, arithmetic and copies ran while one was open for 5% of the time, Pallas kernels for 0%

commit v1 on v0

--- a/solution.py
+++ b/solution.py
@@ -10,7 +10,11 @@
 
 def body(pooled, w_out, assignments, ema_sums, ema_counts):
     partial_value = jnp.dot(pooled, w_out, preferred_element_type=jnp.float32)
-    projected = lax.psum(partial_value, "mp")
+    projected = partial_value
+    for hop in (1, 2):
+        projected = projected + lax.ppermute(
+            projected, "mp", [(dev, dev ^ hop) for dev in range(4)]
+        )
     inverse_norm = 1.0 / jnp.sqrt(jnp.sum(projected * projected, axis=1, keepdims=True) + EPSILON)
     embedded = (projected * inverse_norm).astype(jnp.bfloat16)
     local_centers = ema_sums.shape[0]

time: 216 us -> 314 us (1.45)
  waiting for transfers between devices: 138 us -> 237 us
  starting transfers between devices: 3.87 us -> 9.58 us
    ppermute x0 -> x2, waiting for transfers between devices: none -> 237 us  [body(): lax.ppermute(projected, 'mp', [(dev, dev ^ hop) for dev in range(4)])]
    psum x1 -> x0, waiting for transfers between devices: 138 us -> none  [body(): projected = lax.psum(partial_value, 'mp')]
    ppermute x0 -> x2, starting transfers between devices: none -> 5.94 us  [body(): lax.ppermute(projected, 'mp', [(dev, dev ^ hop) for dev in range(4)])]
  transfers between devices with their start and end apart: 3 -> 4, of which waited for: 1 -> 2; matrix products, arithmetic and copies ran while one was open for 5% -> 5% of each run, Pallas kernels for 0% -> 0%
where the time goes in v1:
time: 314 us
  waiting for transfers between devices  237 us (75%)
  blocking collectives  26.9 us (9%)
  between operations  14.1 us (4%)
  matrix products  11.7 us (4%)
  other arithmetic  10.2 us (3%)
  starting transfers between devices  9.58 us (3%)
  local copies, waits for them, and re-layouts  4.4 us (1%)
    ppermute x2, waiting for transfers between devices, body(): lax.ppermute(projected, 'mp', [(dev, dev ^ hop) for dev in range(4)])  237 us
    all_gather x1, blocking collectives, body(): every_assign = lax.all_gather(assignments, 'dp', axis=0, tiled=True)  26.9 us
  transfers between devices with their start and end apart: 4, of which 2 were waited for; matrix products, arithmetic and copies ran while one was open for 5% of the time, Pallas kernels for 0%

profile of v1, /device:TPU:0, one launch (start us, length us, event | category | flops | bytes accessed | tf_op | source)
XLA Modules:
  0.0 313.6 jit_solution(8445997438360269100)
XLA Ops:
  7.2 0.0 copy-start
  7.2 0.0 all-gather.3.cloned.1.call-start
  7.2 2.7 divide_convert_fusion.1
  9.9 0.0 all-gather.3.cloned.1.call-update
  9.9 0.0 copy-done
  9.9 4.9 %fusion.6 = f32[256,3584]{1,0:T(8,128)S(1)} fusion(bf16[256,896]{1,0:T(8,128)(2,1)S(1)} %copy-done, bf16[896,3584]{1,0:T(8,128)(2,1)} %param.6), kind=kOutput, calls=%fused_computation.18 | convolution fusion | flops 1644167168 | bytes 10551296 | tf_op jit(solution)/shard_map/dot_general | solution.py:12
  14.8 3.1 collective-permute-start
  17.9 79.3 %collective-permute-done = f32[256,3584]{1,0:T(8,128)S(1)} collective-permute-done((f32[256,3584]{1,0:T(8,128)S(1)}, f32[256,3584]{1,0:T(8,128)S(1)}, u32[]{:S(2)}, u32[]{:S(2)}) %collective-permute-start) | collective-permute-done | bytes 3670048 | tf_op jit(solution)/shard_map/ppermute | solution.py:15
  97.3 0.4 add.57
  97.7 2.8 collective-permute-start.1
  100.5 157.3 %collective-permute-done.1 = f32[256,3584]{1,0:T(8,128)S(1)} collective-permute-done((f32[256,3584]{1,0:T(8,128)S(1)}, f32[256,3584]{1,0:T(8,128)S(1)}, u32[]{:S(2)}, u32[]{:S(2)}) %collective-permute-start.1) | collective-permute-done | bytes 3670048 | tf_op jit(solution)/shard_map/ppermute | solution.py:15
  257.8 0.8 multiply_reduce_fusion.2
  258.7 0.6 multiply_reduce_fusion.1
  259.3 0.0 copy-start.2
  259.3 0.0 copy-start.7
  259.3 0.0 copy-start.5
  259.3 2.4 copy.13
  261.7 0.0 copy-done.2
  261.7 3.6 %all-to-all-start = ((bf16[256,8,448]{0,2,1:T(8,128)(2,1)}), bf16[256,8,448]{0,2,1:T(8,128)(2,1)S(1)}, u32[]{:S(2)}, u32[]{:S(2)}) async-start(bf16[256,8,448]{0,2,1:T(8,128)(2,1)} %bitcast.12), calls=%async_computation | async-start | bytes 3670016 | tf_op jit(solution)/shard_map/all_to_all | solution.py:37
  265.4 0.0 copy-done.7
  265.4 26.9 %all-gather = s32[8,1,256]{2,1,0:T(1,128)S(1)} all-gather(s32[1,1,256]{2,1,0:T(1,128)S(1)} %bitcast.16), channel_id=1, replica_groups=mesh['dp'=8,'mp'=4] {'dp'}, dimensions={0}, use_global_device_ids=true | all-gather | bytes 9216 | tf_op jit(solution)/shard_map/all_gather | solution.py:36
  292.2 1.0 convert_reduce_fusion
  293.2 0.0 copy-done.5
  293.2 0.0 copy-start.6
  293.2 0.0 all-to-all-done
  293.2 0.0 copy-start.4
  293.2 0.2 copy.15
  293.5 1.3 copy-done.4
  294.7 0.0 copy-start.3
  294.7 3.8 %divide_convert_fusion = (bf16[1024,448]{0,1:T(8,128)(2,1)}, f32[1024,448]{0,1:T(8,128)}) fusion(f32[1024]{0:T(1024)S(1)} %multiply_add_fusion.1, bf16[2048,448]{0,1:T(8,128)(2,1)S(1)} %bitcast.13, s32[2048]{0:T(1024)S(1)} %bitcast.15, s32[1024]{0:T(1024)S(1)} %iota_add_fusion, f32[1024,448]{0,1:T(8,128)S(1)} %copy-done.4), kind=kOutput, calls=%fused_computation.10 | convolution fusion | flops 1883439104 | bytes 6438912 | tf_op jit(solution)/shard_map/while/body/eval_jaxpr/dot_general | solution.py:52
  298.5 0.0 copy-done.6
  298.5 0.0 all-gather.3.cloned.1.call-done
  298.5 0.0 copy-start.1
  298.5 4.7 %multiply_reduce_fusion = f32[1024]{0:T(1024)S(1)} fusion(bf16[1024,3584]{0,1:T(8,128)(2,1)} %all-gather.3.cloned.1.call-done), kind=kLoop, calls=%fused_computation | loop fusion | flops 11009024 | bytes 7344128 | tf_op jit(solution)/shard_map/reduce_sum | solution.py:28
  303.3 0.0 copy-done.3
  303.3 0.4 copy-done.1
  303.7 3.0 add_subtract_fusion
  (3 shorter events, 0.0 us)
Async XLA Ops:
  7.2 2.8 copy-start
  7.2 291.4 %all-gather.3.cloned.1.call-start = ((), (), s32[]{:S(2)}) async-start(), calls=%async_computation.1 | async-start | bytes 8257536 | tf_op jit(solution)/shard_map/all_gather | solution.py:23
  14.8 82.5 %collective-permute-start = (f32[256,3584]{1,0:T(8,128)S(1)}, f32[256,3584]{1,0:T(8,128)S(1)}, u32[]{:S(2)}, u32[]{:S(2)}) collective-permute-start(f32[256,3584]{1,0:T(8,128)S(1)} %fusion.6), channel_id=1, source_target_pairs={{0,1},{1,0},{2,3},{3,2},{4,5},{5,4},{6,7},{7,6},{8,9},{9,8},{10,11... | collective-permute-start | bytes 11010056 | tf_op jit(solution)/shard_map/ppermute | solution.py:15
  97.7 160.1 %collective-permute-start.1 = (f32[256,3584]{1,0:T(8,128)S(1)}, f32[256,3584]{1,0:T(8,128)S(1)}, u32[]{:S(2)}, u32[]{:S(2)}) collective-permute-start(f32[256,3584]{1,0:T(8,128)S(1)} %add.57), channel_id=1, source_target_pairs={{0,2},{1,3},{2,0},{3,1},{4,6},{5,7},{6,4},{7,5},{8,10},{9,11},{10,... | collective-permute-start | bytes 11010056 | tf_op jit(solution)/shard_map/ppermute | solution.py:15
  259.3 2.5 copy-start.2
  259.3 6.1 %copy-start.7 = (s32[256]{0:T(256)S(1)}, s32[256]{0:T(256)}, u32[]{:S(2)}) copy-start(s32[256]{0:T(256)} %param.7) | copy-start | bytes 3076
  259.3 33.9 %copy-start.5 = (f32[1024]{0:T(1024)S(1)}, f32[1024]{0:T(1024)}, u32[]{:S(2)}) copy-start(f32[1024]{0:T(1024)} %param.9) | copy-start | bytes 12292
  261.7 31.5 %all-to-all-start = ((bf16[256,8,448]{0,2,1:T(8,128)(2,1)}), bf16[256,8,448]{0,2,1:T(8,128)(2,1)S(1)}, u32[]{:S(2)}, u32[]{:S(2)}) async-start(bf16[256,8,448]{0,2,1:T(8,128)(2,1)} %bitcast.12), calls=%async_computation | async-start | bytes 3670016 | tf_op jit(solution)/shard_map/all_to_all | solution.py:37
  293.2 5.3 %copy-start.6 = (f32[1024]{0:T(1024)}, f32[1024]{0:T(1024)S(1)}, u32[]{:S(2)}) copy-start(f32[1024]{0:T(1024)S(1)} %multiply_add_fusion.1) | copy-start | bytes 12292
  293.2 1.5 copy-start.4
  294.7 8.5 %copy-start.3 = (bf16[256,3584]{1,0:T(8,128)(2,1)S(1)}, bf16[256,3584]{1,0:T(8,128)(2,1)}, u32[]{:S(2)}) copy-start(bf16[256,3584]{1,0:T(8,128)(2,1)} %copy-done.2) | copy-start | bytes 5505028
  298.5 5.2 %copy-start.1 = (bf16[1024,3584]{0,1:T(8,128)(2,1)S(1)}, bf16[1024,3584]{0,1:T(8,128)(2,1)}, u32[]{:S(2)}) copy-start(bf16[1024,3584]{0,1:T(8,128)(2,1)} %all-gather.3.cloned.1.call-done) | copy-start | bytes 22020100
Sparse Core Ops, SparseCore 0:
  10.5 52.5 all-gather.2
